TPU v7x, 32 devices: a whole 2x2x4 slice. The times are simulated.
32 devices in a mesh: view: 2 (over y), row: 2 (over x), col: 8 (over z, core).
Axes of the slice: x: 2, y: 2, z: 4, core: 2. Of those that a mesh axis runs over, the one named last changes fastest.
Arguments:
- inputs: bfloat16 [2, 512, 8192], P('view', 'col', 'row'), may hold values from -28 to 28, as said below
- weight: bfloat16 [8192, 8192], P('row', 'col'), may hold values from -0.0625 to 0.0625
Outputs:
- grad_hidden: bfloat16 [2, 512, 8192], P('view', 'col', 'row')
- grad_weight: float32 [8192, 8192], P('row', 'col')
Inputs may be any that keep to these rules, and one draw needn't show every extreme that they name: `inputs`: feature activations of the two views of a clip; each feature has its own scale.
All inputs are finite; a program needn't handle non-finite values.
Results may differ from a plain program's by a relative error of at most 0.025.
Values may be sent and summed in bfloat16 or wider, within the bound.
No kernel may reach another device: no remote copies, remote signals or barrier semaphores. Data moves between devices by JAX's collectives and lax.ppermute only.
A program may use at most 128 MiB of HBM per device.

v0:
```python
import math
import jax
import jax.numpy as jnp
from jax import lax
from jax.sharding import PartitionSpec as P

off_weight = 0.0051
norm_eps = 1e-05


def from_partner(block, axis, distance):
    count = lax.axis_size(axis)
    route = []
    for low in range(count):
        high = low | 1 << distance
        if high != low and high < count:
            route += [(low, high), (high, low)]
    return lax.ppermute(block, axis, route)


def shards(inputs, weight):
    hidden = lax.all_gather(inputs[0], "col", axis=0, tiled=True)
    batch = hidden.shape[0]
    columns = weight
    pre = lax.psum_scatter(
        lax.dot_general(
            columns, hidden, (((0,), (1,)), ((), ())), preferred_element_type=jnp.float32
        ).astype(jnp.bfloat16),
        "row",
        scatter_dimension=0,
        tiled=True,
    ).astype(jnp.float32)
    centred = pre - jnp.mean(pre, axis=1, keepdims=True)
    rstd = lax.rsqrt(jnp.mean(centred * centred, axis=1, keepdims=True) + norm_eps)
    own = (centred * rstd).astype(jnp.bfloat16)
    partner = from_partner(own, "view", 0)
    own_f = own.astype(jnp.float32)
    partner_f = partner.astype(jnp.float32)
    diag = jnp.sum(own_f * partner_f, axis=1, keepdims=True) / batch
    piece = lax.all_gather(partner, ("row", "col"), axis=0, tiled=True)
    corr = (
        lax.dot_general(own, piece, (((1,), (1,)), ((), ())), preferred_element_type=jnp.float32)
        / batch
    )
    mixed = jnp.dot(corr.astype(jnp.bfloat16), piece, preferred_element_type=jnp.float32)
    scale_diag = 2.0 * (diag - 1.0) - 2.0 * off_weight * diag
    dnorm = 2.0 * off_weight * mixed + scale_diag * partner_f
    inner = jnp.mean(dnorm * own_f, axis=1, keepdims=True)
    dpre = (rstd * (dnorm - jnp.mean(dnorm, axis=1, keepdims=True) - own_f * inner)).astype(
        jnp.bfloat16
    )
    grads = lax.all_gather(dpre, "row", axis=0, tiled=True)
    local_weight = lax.dot_general(
        hidden, grads, (((0,), (1,)), ((), ())), preferred_element_type=jnp.float32
    )
    grad_weight = lax.psum(local_weight.astype(jnp.bfloat16), "view").astype(
        jnp.float32
    ) / math.sqrt(2.0 * batch)
    columns = grads
    grad_hidden = lax.psum_scatter(
        lax.dot_general(
            columns, weight, (((0,), (1,)), ((), ())), preferred_element_type=jnp.float32
        ).astype(jnp.bfloat16),
        "col",
        scatter_dimension=0,
        tiled=True,
    )
    return (grad_hidden[None], grad_weight)


def solution(mesh):
    return jax.shard_map(
        shards,
        mesh=mesh,
        in_specs=(P("view", "col", "row"), P("row", "col")),
        out_specs=(P("view", "col", "row"), P("row", "col")),
        check_vma=False,
    )
```

profile of v0, /device:TPU:0, one launch (start us, length us, event | category | flops | bytes accessed | tf_op | source)
XLA Modules:
  0.0 486.3 jit_solution(11138176716313369393)
XLA Ops:
  7.2 0.0 all-gather.9.cloned.1.call-start
  7.2 0.7 all-gather.9.cloned.1.call-update
  7.9 0.0 reduce-scatter.3.cloned.1.call-start
  7.9 51.2 %all-gather.9.cloned.1.call-done = bf16[1,512,4096]{2,1,0:T(8,128)(2,1)} async-done(((bf16[1,64,4096]{2,1,0:T(8,128)(2,1)}), bf16[1,512,4096]{2,1,0:T(8,128)(2,1)}) %all-gather.9.cloned.1.call-update) | async-done | bytes 4194320 | tf_op jit(solution)/shard_map/all_gather | solution.py:22
  59.2 10.1 %fusion.4 = bf16[1024,512]{1,0:T(8,128)(2,1)} fusion(bf16[4096,1024]{1,0:T(8,128)(2,1)} %param.3, bf16[1,512,4096]{2,1,0:T(8,128)(2,1)} %all-gather.9.cloned.1.call-done), kind=kOutput, calls=%fused_computation.11 | convolution fusion | flops 4295491584 | bytes 13631488 | tf_op jit(solution)/shard_map/dot_general | solution.py:26
  69.3 0.0 reduce-scatter.3.cloned.1.call-update
  69.3 0.0 all-gather.5.cloned.1.call-start
  69.4 19.3 %reduce-scatter.3.cloned.1.call-done = bf16[512,512]{1,0:T(8,128)(2,1)} async-done(((bf16[1024,512]{1,0:T(8,128)(2,1)}), bf16[512,512]{1,0:T(8,128)(2,1)}) %reduce-scatter.3.cloned.1.call-update) | async-done | bytes 524304 | tf_op jit(solution)/shard_map/reduce_scatter | solution.py:25
  88.7 1.2 convert_reduce_fusion
  89.9 1.3 fusion.11
  91.2 1.3 fusion.12
  92.5 1.5 collective-permute-start
  94.0 12.0 %collective-permute-done = bf16[512,512]{1,0:T(8,128)(2,1)S(1)} collective-permute-done((bf16[512,512]{1,0:T(8,128)(2,1)S(1)}, bf16[512,512]{1,0:T(8,128)(2,1)S(1)}, u32[]{:S(2)}, u32[]{:S(2)}) %collective-permute-start) | collective-permute-done | bytes 524320 | tf_op jit(solution)/shard_map/ppermute | solution.py:18
  106.0 0.0 copy-start.1
  106.0 0.8 copy-done.1
  106.8 0.0 all-gather.5.cloned.1.call-update
  106.8 0.0 all-gather.7.cloned.1.call-start
  106.9 1.6 fusion.13
  108.5 0.0 copy-start
  108.6 72.7 %all-gather.5.cloned.1.call-done = bf16[8192,512]{1,0:T(8,128)(2,1)} async-done(((bf16[512,512]{1,0:T(8,128)(2,1)}), bf16[8192,512]{1,0:T(8,128)(2,1)}) %all-gather.5.cloned.1.call-update) | async-done | bytes 8388624 | tf_op jit(solution)/shard_map/all_gather | solution.py:40
  181.3 15.2 %fusion.19 = (f32[512]{0:T(512)S(1)}, f32[512]{0:T(512)S(1)}, f32[512,512]{1,0:T(8,128)S(1)}) fusion(bf16[512,512]{1,0:T(8,128)(2,1)S(1)} %fusion.12, bf16[512,512]{1,0:T(8,128)(2,1)} %copy-done.1, f32[512]{0:T(512)S(1)} %multiply_subtract_fusion, bf16[8192,512]{1,0:T(8,128)(2,1)} %all-gather.5.cloned.1.call-done), kind=kOutput, calls=%fused_computation.32 | convolution fusion | flops 8600420352 | bytes 10491904 | tf_op jit(solution)/shard_map/dot_general | solution.py:45
  196.5 0.0 copy-done
  196.6 1.1 fusion.17
  197.7 0.0 all-gather.7.cloned.1.call-update
  197.7 0.2 all-reduce.2.cloned.1.call-start
  197.9 19.8 %all-gather.7.cloned.1.call-done = bf16[1024,512]{1,0:T(8,128)(2,1)} async-done(((bf16[512,512]{1,0:T(8,128)(2,1)}), bf16[1024,512]{1,0:T(8,128)(2,1)}) %all-gather.7.cloned.1.call-update) | async-done | bytes 1048592 | tf_op jit(solution)/shard_map/all_gather | solution.py:52
  217.7 10.4 %convert_bitcast_fusion = bf16[4096,1024]{0,1:T(8,128)(2,1)} fusion(bf16[1024,512]{1,0:T(8,128)(2,1)} %all-gather.7.cloned.1.call-done, bf16[1,512,4096]{2,1,0:T(8,128)(2,1)} %all-gather.9.cloned.1.call-done), kind=kOutput, calls=%fused_computation.2 | convolution fusion | flops 4299161600 | bytes 13631488 | tf_op jit(solution)/shard_map/dot_general | solution.py:53
  228.2 0.0 copy-start.2
  228.2 0.0 all-reduce.2.cloned.1.call-update
  228.2 0.0 reduce-scatter.5.cloned.1.call-start
  228.2 1.1 copy-done.2
  229.4 9.6 %convolution_convert_fusion = bf16[512,4096]{1,0:T(8,128)(2,1)} fusion(bf16[1024,512]{1,0:T(8,128)(2,1)S(1)} %copy-done.2, bf16[4096,1024]{1,0:T(8,128)(2,1)} %param.3), kind=kOutput, calls=%fused_computation.3 | convolution fusion | flops 4297064448 | bytes 13631488 | tf_op jit(solution)/shard_map/dot_general | solution.py:61
  239.0 0.0 reduce-scatter.5.cloned.1.call-update
  239.0 187.4 %all-reduce.2.cloned.1.call-done = bf16[4096,1024]{0,1:T(8,128)(2,1)} async-done(((bf16[4096,1024]{0,1:T(8,128)(2,1)}), bf16[4096,1024]{0,1:T(8,128)(2,1)}) %all-reduce.2.cloned.1.call-update) | async-done | bytes 8388624 | tf_op jit(solution)/shard_map/psum | solution.py:56
  426.4 11.7 %convert_multiply_fusion = f32[4096,1024]{0,1:T(8,128)} fusion(bf16[4096,1024]{0,1:T(8,128)(2,1)} %all-reduce.2.cloned.1.call-done), kind=kLoop, calls=%fused_computation | loop fusion | flops 8388608 | bytes 25165824 | tf_op jit(solution)/shard_map/div | solution.py:56
  438.1 17.5 %copy.5 = f32[4096,1024]{1,0:T(8,128)} copy(f32[4096,1024]{0,1:T(8,128)} %convert_multiply_fusion) | data formatting | bytes 33554432
  455.6 23.8 %reduce-scatter.5.cloned.1.call-done = bf16[64,4096]{1,0:T(8,128)(2,1)} async-done(((bf16[512,4096]{1,0:T(8,128)(2,1)}), bf16[64,4096]{1,0:T(8,128)(2,1)}) %reduce-scatter.5.cloned.1.call-update) | async-done | bytes 524304 | tf_op jit(solution)/shard_map/reduce_scatter | solution.py:60
  (4 shorter events, 0.0 us)
Async XLA Ops:
  7.2 52.0 %all-gather.9.cloned.1.call-start = ((), (), s32[]{:S(2)}) async-start(), calls=%async_computation.7 | async-start | bytes 4718592 | tf_op jit(solution)/shard_map/all_gather | solution.py:22
  7.9 80.8 %reduce-scatter.3.cloned.1.call-start = ((), (), s32[]{:S(2)}) async-start(), calls=%async_computation.2 | async-start | bytes 1572864 | tf_op jit(solution)/shard_map/reduce_scatter | solution.py:25
  69.3 112.0 %all-gather.5.cloned.1.call-start = ((), (), s32[]{:S(2)}) async-start(), calls=%async_computation.3 | async-start | bytes 8912896 | tf_op jit(solution)/shard_map/all_gather | solution.py:40
  92.5 13.6 %collective-permute-start = (bf16[512,512]{1,0:T(8,128)(2,1)S(1)}, bf16[512,512]{1,0:T(8,128)(2,1)S(1)}, u32[]{:S(2)}, u32[]{:S(2)}) collective-permute-start(bf16[512,512]{1,0:T(8,128)(2,1)S(1)} %fusion.12), channel_id=1, source_target_pairs={{0,16},{16,0},{1,17},{17,1},{2,18},{18,2},{3,19},{19,3},{4,20},{20... | collective-permute-start | bytes 1572872 | tf_op jit(solution)/shard_map/ppermute | solution.py:18
  106.0 0.8 copy-start.1
  106.8 110.9 %all-gather.7.cloned.1.call-start = ((), (), s32[]{:S(2)}) async-start(), calls=%async_computation.4 | async-start | bytes 1572864 | tf_op jit(solution)/shard_map/all_gather | solution.py:52
  108.5 88.0 %copy-start = (bf16[512,512]{1,0:T(8,128)(2,1)S(1)}, bf16[512,512]{1,0:T(8,128)(2,1)}, u32[]{:S(2)}) copy-start(bf16[512,512]{1,0:T(8,128)(2,1)} %reduce-scatter.3.cloned.1.call-done) | copy-start | bytes 1572868
  197.7 228.7 %all-reduce.2.cloned.1.call-start = ((), (), s32[]{:S(2)}) async-start(), calls=%async_computation.6 | async-start | bytes 16777216 | tf_op jit(solution)/shard_map/psum | solution.py:56
  228.2 1.2 copy-start.2
  228.2 251.2 %reduce-scatter.5.cloned.1.call-start = ((), (), s32[]{:S(2)}) async-start(), calls=%async_computation.5 | async-start | bytes 4718592 | tf_op jit(solution)/shard_map/reduce_scatter | solution.py:60
Sparse Core Ops, SparseCore 0:
  9.6 49.5 all-gather.8
  69.4 19.1 reduce-scatter.2
  107.0 74.2 all-gather.4
  197.8 19.8 all-gather.6
  228.3 198.0 all-reduce.1
  429.1 50.2 reduce-scatter.4
where the time goes:
time: 487 us; the launch traced here: 486 us
  waiting for transfers between devices  387 us (79%)
  matrix products  45.4 us (9%)
  local copies, waits for them, and re-layouts  19.5 us (4%)
  other arithmetic  18.3 us (4%)
  between operations  14.2 us (3%)
    psum x1, waiting for transfers between devices, shards(): lax.psum(local_weight.astype(jnp.bfloat16), 'view').astype(jnp.float32)  187 us
    all_gather x1, waiting for transfers between devices, shards(): piece = lax.all_gather(partner, ('row', 'col'), axis=0, tiled=True)  72.7 us
    all_gather x1, waiting for transfers between devices, shards(): hidden = lax.all_gather(inputs[0], 'col', axis=0, tiled=True)  51.2 us
    reduce_scatter x1, waiting for transfers between devices, shards(): lax.psum_scatter(lax.dot_general(columns, weight, (((0,), (1,)), ((), ())...  23.8 us
    all_gather x1, waiting for transfers between devices, shards(): grads = lax.all_gather(dpre, 'row', axis=0, tiled=True)  19.8 us
    unnamed x7, local copies, waits for them, and re-layouts  19.5 us
    reduce_scatter x1, waiting for transfers between devices, shards(): lax.psum_scatter(lax.dot_general(columns, hidden, (((0,), (1,)), ((), ())...  19.3 us
    dot_general x1, matrix products, shards(): jnp.dot(corr.astype(jnp.bfloat16), piece, preferred_element_type=jnp.floa...  15.2 us
  transfers between devices with their start and end apart: 7, of which 7 were waited for; matrix products, arithmetic and copies ran while one was open for 8% of the time, Pallas kernels for 0%

commit v1 on v0

--- a/solution.py
+++ b/solution.py
@@ -53,7 +53,7 @@
     local_weight = lax.dot_general(
         hidden, grads, (((0,), (1,)), ((), ())), preferred_element_type=jnp.float32
     )
-    grad_weight = lax.psum(local_weight.astype(jnp.bfloat16), "view").astype(
+    grad_weight = jnp.sum(lax.all_gather(local_weight.astype(jnp.bfloat16), "view"), axis=0).astype(
         jnp.float32
     ) / math.sqrt(2.0 * batch)
     columns = grads

time: 487 us -> 539 us (1.11)
  other arithmetic: 18.3 us -> 65.3 us
  local copies, waits for them, and re-layouts: 19.5 us -> 47.2 us
  waiting for transfers between devices: 387 us -> 364 us
    all_gather x0 -> x1, waiting for transfers between devices: none -> 188 us  [shards(): lax.all_gather(local_weight.astype(jnp.bfloat16), 'view')]
    psum x1 -> x0, waiting for transfers between devices: 187 us -> none  [shards(): lax.psum(local_weight.astype(jnp.bfloat16), 'view').astype(jnp.float32)]
    reduce_sum x0 -> x1, other arithmetic: none -> 47.2 us  [shards(): jnp.sum(lax.all_gather(local_weight.astype(jnp.bfloat16), 'view'), axis=0)]
    all_gather x0 -> x1, local copies, waits for them, and re-layouts: none -> 27.8 us  [shards(): lax.all_gather(local_weight.astype(jnp.bfloat16), 'view')]
    reduce_scatter x1, waiting for transfers between devices: 23.8 us -> 0.01 us  [shards(): lax.psum_scatter(lax.dot_general(columns, weight, (((0,), (1,)), ((), ())...]
  transfers between devices with their start and end apart: 7 -> 7, of which waited for: 7 -> 6; matrix products, arithmetic and copies ran while one was open for 8% -> 21% of each run, Pallas kernels for 0% -> 0%
where the time goes in v1:
time: 539 us; the launch traced here: 538 us
  waiting for transfers between devices  364 us (68%)
  other arithmetic  65.3 us (12%)
  local copies, waits for them, and re-layouts  47.2 us (9%)
  matrix products  45.7 us (8%)
  between operations  14.2 us (3%)
    all_gather x1, waiting for transfers between devices, shards(): lax.all_gather(local_weight.astype(jnp.bfloat16), 'view')  188 us
    all_gather x1, waiting for transfers between devices, shards(): piece = lax.all_gather(partner, ('row', 'col'), axis=0, tiled=True)  72.7 us
    all_gather x1, waiting for transfers between devices, shards(): hidden = lax.all_gather(inputs[0], 'col', axis=0, tiled=True)  51.2 us
    reduce_sum x1, other arithmetic, shards(): jnp.sum(lax.all_gather(local_weight.astype(jnp.bfloat16), 'view'), axis=0)  47.2 us
    all_gather x1, local copies, waits for them, and re-layouts, shards(): lax.all_gather(local_weight.astype(jnp.bfloat16), 'view')  27.8 us
    all_gather x1, waiting for transfers between devices, shards(): grads = lax.all_gather(dpre, 'row', axis=0, tiled=True)  19.8 us
    unnamed x7, local copies, waits for them, and re-layouts  19.4 us
    reduce_scatter x1, waiting for transfers between devices, shards(): lax.psum_scatter(lax.dot_general(columns, hidden, (((0,), (1,)), ((), ())...  19.3 us
  transfers between devices with their start and end apart: 7, of which 6 were waited for; matrix products, arithmetic and copies ran while one was open for 21% of the time, Pallas kernels for 0%

profile of v1, /device:TPU:0, one launch (start us, length us, event | category | flops | bytes accessed | tf_op | source)
XLA Modules:
  0.0 538.0 jit_solution(6109151824123598792)
XLA Ops:
  7.2 0.0 all-gather.11.cloned.1.call-start
  7.2 0.7 all-gather.11.cloned.1.call-update
  7.9 0.0 reduce-scatter.3.cloned.1.call-start
  7.9 51.2 %all-gather.11.cloned.1.call-done = bf16[1,512,4096]{2,1,0:T(8,128)(2,1)} async-done(((bf16[1,64,4096]{2,1,0:T(8,128)(2,1)}), bf16[1,512,4096]{2,1,0:T(8,128)(2,1)}) %all-gather.11.cloned.1.call-update) | async-done | bytes 4194320 | tf_op jit(solution)/shard_map/all_gather | solution.py:22
  59.2 10.1 %fusion.4 = bf16[1024,512]{1,0:T(8,128)(2,1)} fusion(bf16[4096,1024]{1,0:T(8,128)(2,1)} %param.3, bf16[1,512,4096]{2,1,0:T(8,128)(2,1)} %all-gather.11.cloned.1.call-done), kind=kOutput, calls=%fused_computation.11 | convolution fusion | flops 4295491584 | bytes 13631488 | tf_op jit(solution)/shard_map/dot_general | solution.py:26
  69.3 0.0 reduce-scatter.3.cloned.1.call-update
  69.3 0.0 all-gather.7.cloned.1.call-start
  69.4 19.3 %reduce-scatter.3.cloned.1.call-done = bf16[512,512]{1,0:T(8,128)(2,1)} async-done(((bf16[1024,512]{1,0:T(8,128)(2,1)}), bf16[512,512]{1,0:T(8,128)(2,1)}) %reduce-scatter.3.cloned.1.call-update) | async-done | bytes 524304 | tf_op jit(solution)/shard_map/reduce_scatter | solution.py:25
  88.7 1.2 convert_reduce_fusion
  89.9 1.3 fusion.11
  91.2 1.3 fusion.12
  92.5 1.5 collective-permute-start
  94.0 12.0 %collective-permute-done = bf16[512,512]{1,0:T(8,128)(2,1)S(1)} collective-permute-done((bf16[512,512]{1,0:T(8,128)(2,1)S(1)}, bf16[512,512]{1,0:T(8,128)(2,1)S(1)}, u32[]{:S(2)}, u32[]{:S(2)}) %collective-permute-start) | collective-permute-done | bytes 524320 | tf_op jit(solution)/shard_map/ppermute | solution.py:18
  106.0 0.0 copy-start.1
  106.0 0.8 copy-done.1
  106.8 0.0 all-gather.7.cloned.1.call-update
  106.8 0.0 all-gather.9.cloned.1.call-start
  106.9 1.6 fusion.13
  108.5 0.0 copy-start
  108.6 72.7 %all-gather.7.cloned.1.call-done = bf16[8192,512]{1,0:T(8,128)(2,1)} async-done(((bf16[512,512]{1,0:T(8,128)(2,1)}), bf16[8192,512]{1,0:T(8,128)(2,1)}) %all-gather.7.cloned.1.call-update) | async-done | bytes 8388624 | tf_op jit(solution)/shard_map/all_gather | solution.py:40
  181.3 15.2 %fusion.19 = (f32[512]{0:T(512)S(1)}, f32[512]{0:T(512)S(1)}, f32[512,512]{1,0:T(8,128)S(1)}) fusion(bf16[512,512]{1,0:T(8,128)(2,1)S(1)} %fusion.12, bf16[512,512]{1,0:T(8,128)(2,1)} %copy-done.1, f32[512]{0:T(512)S(1)} %multiply_subtract_fusion, bf16[8192,512]{1,0:T(8,128)(2,1)} %all-gather.7.cloned.1.call-done), kind=kOutput, calls=%fused_computation.32 | convolution fusion | flops 8600420352 | bytes 10491904 | tf_op jit(solution)/shard_map/dot_general | solution.py:45
  196.5 0.0 copy-done
  196.5 1.1 fusion.17
  197.7 0.0 all-gather.9.cloned.1.call-update
  197.7 0.2 all-gather.13.cloned.1.call-start
  197.9 19.8 %all-gather.9.cloned.1.call-done = bf16[1024,512]{1,0:T(8,128)(2,1)} async-done(((bf16[512,512]{1,0:T(8,128)(2,1)}), bf16[1024,512]{1,0:T(8,128)(2,1)}) %all-gather.9.cloned.1.call-update) | async-done | bytes 1048592 | tf_op jit(solution)/shard_map/all_gather | solution.py:52
  217.7 10.4 %convert_bitcast_fusion = bf16[4096,1024]{0,1:T(8,128)(2,1)} fusion(bf16[1024,512]{1,0:T(8,128)(2,1)} %all-gather.9.cloned.1.call-done, bf16[1,512,4096]{2,1,0:T(8,128)(2,1)} %all-gather.11.cloned.1.call-done), kind=kOutput, calls=%fused_computation.2 | convolution fusion | flops 4299161600 | bytes 13631488 | tf_op jit(solution)/shard_map/dot_general | solution.py:53
  228.2 0.0 copy-start.2
  228.2 0.0 all-gather.13.cloned.1.call-update
  228.2 0.0 reduce-scatter.5.cloned.1.call-start
  228.2 1.1 copy-done.2
  229.4 9.9 %convolution_convert_fusion = bf16[512,4096]{1,0:T(8,128)(2,1)} fusion(bf16[1024,512]{1,0:T(8,128)(2,1)S(1)} %copy-done.2, bf16[4096,1024]{1,0:T(8,128)(2,1)} %param.3), kind=kOutput, calls=%fused_computation.3 | convolution fusion | flops 4297064448 | bytes 13631488 | tf_op jit(solution)/shard_map/dot_general | solution.py:61
  239.3 0.0 reduce-scatter.5.cloned.1.call-update
  239.3 187.8 %all-gather.13.cloned.1.call-done = bf16[8192,1024]{0,1:T(8,128)(2,1)} async-done(((bf16[4096,1024]{0,1:T(8,128)(2,1)}), bf16[8192,1024]{0,1:T(8,128)(2,1)}) %all-gather.13.cloned.1.call-update) | async-done | bytes 16777232 | tf_op jit(solution)/shard_map/all_gather | solution.py:56
  427.2 27.8 %reshape.37 = bf16[2,4096,1024]{1,0,2:T(2,128)(2,1)} reshape(bf16[8192,1024]{0,1:T(8,128)(2,1)} %all-gather.13.cloned.1.call-done) | data formatting | bytes 33554432 | tf_op jit(solution)/shard_map/all_gather | solution.py:56
  455.0 47.2 %reduce_sum.62 = bf16[4096,1024]{0,1:T(8,128)(2,1)} reduce(bf16[2,4096,1024]{1,0,2:T(2,128)(2,1)} %reshape.37, bf16[]{:T(256)} %constant.26.clone.1), dimensions={0}, to_apply=%region_7.0 | reduce | flops 4194304 | bytes 25165826 | tf_op jit(solution)/shard_map/reduce_sum | solution.py:56
  502.2 11.5 %convert_multiply_fusion = f32[4096,1024]{0,1:T(8,128)} fusion(bf16[4096,1024]{0,1:T(8,128)(2,1)} %reduce_sum.62), kind=kLoop, calls=%fused_computation | loop fusion | flops 8388608 | bytes 25165824 | tf_op jit(solution)/shard_map/div | solution.py:56
  513.7 17.4 %copy.6 = f32[4096,1024]{1,0:T(8,128)} copy(f32[4096,1024]{0,1:T(8,128)} %convert_multiply_fusion) | data formatting | bytes 33554432
  531.1 0.0 reduce-scatter.5.cloned.1.call-done
  (4 shorter events, 0.0 us)
Async XLA Ops:
  7.2 52.0 %all-gather.11.cloned.1.call-start = ((), (), s32[]{:S(2)}) async-start(), calls=%async_computation.6 | async-start | bytes 4718592 | tf_op jit(solution)/shard_map/all_gather | solution.py:22
  7.9 80.8 %reduce-scatter.3.cloned.1.call-start = ((), (), s32[]{:S(2)}) async-start(), calls=%async_computation.2 | async-start | bytes 1572864 | tf_op jit(solution)/shard_map/reduce_scatter | solution.py:25
  69.3 112.0 %all-gather.7.cloned.1.call-start = ((), (), s32[]{:S(2)}) async-start(), calls=%async_computation.3 | async-start | bytes 8912896 | tf_op jit(solution)/shard_map/all_gather | solution.py:40
  92.5 13.6 %collective-permute-start = (bf16[512,512]{1,0:T(8,128)(2,1)S(1)}, bf16[512,512]{1,0:T(8,128)(2,1)S(1)}, u32[]{:S(2)}, u32[]{:S(2)}) collective-permute-start(bf16[512,512]{1,0:T(8,128)(2,1)S(1)} %fusion.12), channel_id=1, source_target_pairs={{0,16},{16,0},{1,17},{17,1},{2,18},{18,2},{3,19},{19,3},{4,20},{20... | collective-permute-start | bytes 1572872 | tf_op jit(solution)/shard_map/ppermute | solution.py:18
  106.0 0.8 copy-start.1
  106.8 110.9 %all-gather.9.cloned.1.call-start = ((), (), s32[]{:S(2)}) async-start(), calls=%async_computation.4 | async-start | bytes 1572864 | tf_op jit(solution)/shard_map/all_gather | solution.py:52
  108.5 88.0 %copy-start = (bf16[512,512]{1,0:T(8,128)(2,1)S(1)}, bf16[512,512]{1,0:T(8,128)(2,1)}, u32[]{:S(2)}) copy-start(bf16[512,512]{1,0:T(8,128)(2,1)} %reduce-scatter.3.cloned.1.call-done) | copy-start | bytes 1572868
  197.7 229.5 %all-gather.13.cloned.1.call-start = ((), (), s32[]{:S(2)}) async-start(), calls=%async_computation.7 | async-start | bytes 25165824 | tf_op jit(solution)/shard_map/all_gather | solution.py:56
  228.2 1.2 copy-start.2
  228.2 302.9 %reduce-scatter.5.cloned.1.call-start = ((), (), s32[]{:S(2)}) async-start(), calls=%async_computation.5 | async-start | bytes 4718592 | tf_op jit(solution)/shard_map/reduce_scatter | solution.py:60
Sparse Core Ops, SparseCore 0:
  9.6 49.5 all-gather.10
  69.4 19.1 reduce-scatter.2
  107.0 74.2 all-gather.6
  197.8 19.8 all-gather.8
  228.3 198.8 all-gather.12
  429.9 49.8 reduce-scatter.4
